TPU v7x, 256 devices: a whole 4x4x8 slice. The times are simulated.
256 devices in a mesh: dp: 16 (over z, x_hi), tensor: 16 (over x_lo, y, core).
Axes of the slice: x: 4 (x_hi: 2, x_lo: 2; x = x_hi * 2 + x_lo), y: 4, z: 8, core: 2. Of those that a mesh axis runs over, the one named last changes fastest.
Arguments:
- inputs: bfloat16 [8192, 2304], P(('dp', 'tensor')), may hold values from -6 to 6
- out_grad: bfloat16 [8192, 2304], P(('dp', 'tensor')), may hold values from -0.59765625 to 0.59765625
- gate_pre: bfloat16 [8192, 18432], P('dp', 'tensor'), may hold values from -6 to 6
- up_pre: bfloat16 [8192, 18432], P('dp', 'tensor'), may hold values from -6 to 6
- w_down: bfloat16 [18432, 2304], P('tensor'), may hold values from -0.046875 to 0.046875
- proj_new: bfloat16 [2304, 3, 256], replicated, may hold values from -0.125 to 0.125
- proj_old: bfloat16 [2304, 3, 256], P('tensor'), may hold values from -0.125 to 0.125
- first_old: float32 [256, 3, 18432], P('dp', None, 'tensor'), may hold values from -6 to 6
- second_old: float32 [256, 3, 18432], P('dp', None, 'tensor'), may hold values from 0.1 to 10
Outputs:
- first_new: float32 [256, 3, 18432], P('dp', None, 'tensor')
- second_new: float32 [256, 3, 18432], P('dp', None, 'tensor')
All inputs are finite; a program needn't handle non-finite values.
Results may differ from a plain program's by a relative error of at most 0.0005.
Values may be sent and summed in bfloat16 or wider, within the bound.
A program may use at most 64 MiB of HBM per device.

v0:
```python
import jax
import jax.numpy as jnp
from jax import lax
from jax.sharding import PartitionSpec as P

coeff = 0.7978845608028654


def gelu_pair(gate):
    inner = coeff * (gate + 0.044715 * gate * gate * gate)
    tval = jnp.tanh(inner)
    value = 0.5 * gate * (1.0 + tval)
    slope = 0.5 * (1.0 + tval) + 0.5 * gate * (1.0 - tval * tval) * coeff * (
        1.0 + 3.0 * 0.044715 * gate * gate
    )
    return (value, slope)


def on_device(
    inputs, out_grad, gate_pre, up_pre, w_down, proj_new, proj_old, first_old, second_old
):
    width = proj_new.shape[0]
    rank = proj_new.shape[2]
    flat = proj_new.reshape(width, 3 * rank)
    in_side = flat[:, : 2 * rank]
    out_side = flat[:, 2 * rank :]
    slab = width // lax.axis_size("tensor")
    own_new = lax.dynamic_slice_in_dim(proj_new, lax.axis_index("tensor") * slab, slab, 0)
    partial_rot = jnp.einsum("dki,dkj->kij", own_new, proj_old, preferred_element_type=jnp.float32)
    rotation = lax.psum(partial_rot, "tensor")
    in_proj = jnp.dot(
        lax.all_gather(inputs, "tensor", axis=0, tiled=True),
        in_side,
        preferred_element_type=jnp.float32,
    ).astype(jnp.bfloat16)
    piece = lax.all_gather(out_grad, "tensor", axis=0, tiled=True)
    hidden_rows = lax.dot_general(
        piece, w_down, (((1,), (1,)), ((), ())), preferred_element_type=jnp.float32
    )
    out_rows = jnp.dot(piece, out_side, preferred_element_type=jnp.float32).astype(jnp.bfloat16)
    value, slope = gelu_pair(gate_pre.astype(jnp.float32))
    up_rows = up_pre.astype(jnp.float32)
    gate_grad = (hidden_rows * up_rows * slope).astype(jnp.bfloat16)
    up_grad = (hidden_rows * value).astype(jnp.bfloat16)
    hidden = (value * up_rows).astype(jnp.bfloat16)
    contract = (((0,), (0,)), ((), ()))
    low_gate = lax.dot_general(
        in_proj[:, :rank], gate_grad, contract, preferred_element_type=jnp.float32
    )
    low_up = lax.dot_general(
        in_proj[:, rank:], up_grad, contract, preferred_element_type=jnp.float32
    )
    low_down = lax.dot_general(out_rows, hidden, contract, preferred_element_type=jnp.float32)
    low_grad = jnp.stack([low_gate, low_up, low_down], axis=1)
    full_first, full_second = (
        lax.all_gather(first_old, "dp", axis=0, tiled=True),
        lax.all_gather(second_old, "dp", axis=0, tiled=True),
    )
    summed = lax.psum_scatter(low_grad, "dp", scatter_dimension=0, tiled=True)
    share = first_old.shape[0]
    rot_rows = lax.dynamic_slice_in_dim(rotation, lax.axis_index("dp") * share, share, 1)
    turned_first = jnp.einsum("kij,jkc->ikc", rot_rows, full_first, precision=lax.Precision.HIGHEST)
    turned_second = jnp.einsum(
        "kij,jkc->ikc", rot_rows * rot_rows, full_second, precision=lax.Precision.HIGHEST
    )
    first_new = 0.9 * turned_first + 0.1 * summed
    second_new = 0.999 * turned_second + 0.001 * summed * summed
    return (first_new, second_new)


def solution(mesh):
    placed = (
        P(("dp", "tensor"), None),
        P(("dp", "tensor"), None),
        P("dp", "tensor"),
        P("dp", "tensor"),
        P("tensor", None),
        P(),
        P("tensor", None, None),
        P("dp", None, "tensor"),
        P("dp", None, "tensor"),
    )
    return jax.shard_map(
        on_device,
        mesh=mesh,
        in_specs=placed,
        out_specs=(P("dp", None, "tensor"), P("dp", None, "tensor")),
        check_vma=False,
    )
```

profile of v0, /device:TPU:8, one launch (start us, length us, event | category | flops | bytes accessed | tf_op | source)
XLA Modules:
  0.0 635.6 jit_solution(3412581405455012115)
XLA Ops:
  7.2 0.0 copy-start
  7.2 0.0 all-gather.7.cloned.1.call-start
  7.2 0.7 all-gather.7.cloned.1.call-update
  7.9 0.0 all-gather.9.cloned.1.call-start
  8.0 0.7 all-gather.9.cloned.1.call-update
  8.7 0.0 all-reduce.2.cloned.1.call-start
  8.7 0.0 copy-done
  8.7 2.2 fusion.27
  10.9 0.0 all-reduce.2.cloned.1.call-update
  11.0 0.0 all-gather.11.cloned.1.call-start
  11.0 0.5 all-gather.11.cloned.1.call-update
  11.5 0.0 reduce-scatter.2.cloned.1.call-start
  11.6 5.8 copy.11
  17.4 31.7 %all-gather.7.cloned.1.call-done = bf16[512,2304]{1,0:T(8,128)(2,1)} async-done(((bf16[32,2304]{1,0:T(8,128)(2,1)}), bf16[512,2304]{1,0:T(8,128)(2,1)}) %all-gather.7.cloned.1.call-update) | async-done | bytes 2359312 | tf_op jit(solution)/shard_map/all_gather | solution.py:32
  49.2 3.8 fusion.17
  53.0 0.0 copy-start.2
  53.0 34.8 %all-gather.9.cloned.1.call-done = bf16[512,2304]{1,0:T(8,128)(2,1)} async-done(((bf16[32,2304]{1,0:T(8,128)(2,1)}), bf16[512,2304]{1,0:T(8,128)(2,1)}) %all-gather.9.cloned.1.call-update) | async-done | bytes 2359312 | tf_op jit(solution)/shard_map/all_gather | solution.py:36
  87.8 6.5 %fusion.48 = f32[512,1152]{1,0:T(8,128)S(1)} fusion(bf16[512,2304]{1,0:T(8,128)(2,1)} %all-gather.9.cloned.1.call-done, bf16[1152,2304]{1,0:T(8,128)(2,1)} %param.13), kind=kOutput, calls=%fused_computation.60 | convolution fusion | flops 2717908992 | bytes 10027008 | tf_op jit(solution)/shard_map/dot_general | solution.py:37
  94.3 0.0 copy-start.3
  94.3 1.4 copy-done.3
  95.7 0.0 copy-done.2
  95.7 1.2 convolution_bitcast_fusion.1
  96.9 4.8 convolution_bitcast_fusion
  101.7 4.3 convolution_bitcast_fusion.2
  106.0 2.1 pad_maximum_fusion
  108.1 0.0 reduce-scatter.2.cloned.1.call-update
  108.2 0.2 all-gather.5.cloned.1.call-start
  108.4 0.3 all-gather.5.cloned.1.call-update
  108.7 103.4 %all-reduce.2.cloned.1.call-done = f32[3,256,256]{2,1,0:T(8,128)} async-done(((f32[3,256,256]{2,1,0:T(8,128)}), f32[3,256,256]{2,1,0:T(8,128)}) %all-reduce.2.cloned.1.call-update) | async-done | bytes 786448 | tf_op jit(solution)/shard_map/psum | solution.py:30
  212.1 102.2 %all-gather.11.cloned.1.call-done = f32[256,3,1152]{2,0,1:T(8,128)} async-done(((f32[16,3,1152]{2,0,1:T(8,128)}), f32[256,3,1152]{2,0,1:T(8,128)}) %all-gather.11.cloned.1.call-update) | async-done | bytes 3538960 | tf_op jit(solution)/shard_map/all_gather | solution.py:57
  314.3 214.0 %reduce-scatter.2.cloned.1.call-done = f32[16,3,1152]{2,0,1:T(8,128)} async-done(((f32[256,3,1152]{2,0,1:T(8,128)}), f32[16,3,1152]{2,0,1:T(8,128)}) %reduce-scatter.2.cloned.1.call-update) | async-done | bytes 221200 | tf_op jit(solution)/shard_map/reduce_scatter | solution.py:59
  528.3 0.0 copy-start.1
  528.3 4.5 fusion.16
  532.9 91.3 %all-gather.5.cloned.1.call-done = f32[256,3,1152]{2,0,1:T(8,128)} async-done(((f32[16,3,1152]{2,0,1:T(8,128)}), f32[256,3,1152]{2,0,1:T(8,128)}) %all-gather.5.cloned.1.call-update) | async-done | bytes 3538960 | tf_op jit(solution)/shard_map/all_gather | solution.py:56
  624.2 0.0 copy-done.1
  624.2 4.5 fusion.14
Async XLA Ops:
  7.2 1.6 copy-start
  7.2 42.0 %all-gather.7.cloned.1.call-start = ((), (), s32[]{:S(2)}) async-start(), calls=%async_computation.3 | async-start | bytes 2506752 | tf_op jit(solution)/shard_map/all_gather | solution.py:32
  7.9 79.9 %all-gather.9.cloned.1.call-start = ((), (), s32[]{:S(2)}) async-start(), calls=%async_computation.4 | async-start | bytes 2506752 | tf_op jit(solution)/shard_map/all_gather | solution.py:36
  8.7 203.5 %all-reduce.2.cloned.1.call-start = ((), (), s32[]{:S(2)}) async-start(), calls=%async_computation.1 | async-start | bytes 1572864 | tf_op jit(solution)/shard_map/psum | solution.py:30
  11.0 303.4 %all-gather.11.cloned.1.call-start = ((), (), s32[]{:S(2)}) async-start(), calls=%async_computation.6 | async-start | bytes 3760128 | tf_op jit(solution)/shard_map/all_gather | solution.py:57
  11.5 516.8 %reduce-scatter.2.cloned.1.call-start = ((), (), s32[]{:S(2)}) async-start(), calls=%async_computation.5 | async-start | bytes 3760128 | tf_op jit(solution)/shard_map/reduce_scatter | solution.py:59
  53.0 42.7 %copy-start.2 = (bf16[512,1152]{1,0:T(8,128)(2,1)S(1)}, bf16[512,1152]{1,0:T(8,128)(2,1)}, u32[]{:S(2)}) copy-start(bf16[512,1152]{1,0:T(8,128)(2,1)} %param.11) | copy-start | bytes 3538948
  94.3 1.4 copy-start.3
  108.2 516.0 %all-gather.5.cloned.1.call-start = ((), (), s32[]{:S(2)}) async-start(), calls=%async_computation.2 | async-start | bytes 3760128 | tf_op jit(solution)/shard_map/all_gather | solution.py:56
  528.3 95.9 %copy-start.1 = (f32[16,3,1152]{2,0,1:T(8,128)S(1)}, f32[16,3,1152]{2,0,1:T(8,128)}, u32[]{:S(2)}) copy-start(f32[16,3,1152]{2,0,1:T(8,128)} %reduce-scatter.2.cloned.1.call-done) | copy-start | bytes 663556
Sparse Core Ops, SparseCore 0:
  9.8 39.2 all-gather.6
  51.0 36.7 all-gather.8
  90.4 121.6 all-reduce.1
  214.6 99.6 all-gather.10
  318.2 210.0 reduce-scatter.1
  530.8 93.3 all-gather.4
where the time goes:
time: 636 us
  waiting for transfers between devices  580 us (91%)
  matrix products  31.9 us (5%)
  between operations  14.2 us (2%)
  local copies, waits for them, and re-layouts  7.26 us (1%)
    reduce_scatter x1, waiting for transfers between devices, on_device(): summed = lax.psum_scatter(low_grad, 'dp', scatter_dimension=0, tiled=True)  214 us
    psum x1, waiting for transfers between devices, on_device(): rotation = lax.psum(partial_rot, 'tensor')  103 us
    all_gather x1, waiting for transfers between devices, on_device(): lax.all_gather(second_old, 'dp', axis=0, tiled=True)  102 us
    all_gather x1, waiting for transfers between devices, on_device(): lax.all_gather(first_old, 'dp', axis=0, tiled=True)  91.3 us
    all_gather x1, waiting for transfers between devices, on_device(): piece = lax.all_gather(out_grad, 'tensor', axis=0, tiled=True)  34.8 us
    all_gather x1, waiting for transfers between devices, on_device(): lax.all_gather(inputs, 'tensor', axis=0, tiled=True)  31.7 us
  transfers between devices with their start and end apart: 6, of which 6 were waited for; matrix products, arithmetic and copies ran while one was open for 6% of the time, Pallas kernels for 0%

commit v1 on v0

--- a/solution.py
+++ b/solution.py
@@ -4,6 +4,13 @@
 from jax.sharding import PartitionSpec as P
 
 coeff = 0.7978845608028654
+
+
+def all_by_exchange(block, axis, dim):
+    size = lax.axis_size(axis)
+    blocks = jnp.stack([block for _ in range(size)])
+    blocks = lax.all_to_all(blocks, axis, split_axis=0, concat_axis=0)
+    return jnp.concatenate(blocks, axis=dim)
 
 
 def gelu_pair(gate):
@@ -29,9 +36,7 @@
     partial_rot = jnp.einsum("dki,dkj->kij", own_new, proj_old, preferred_element_type=jnp.float32)
     rotation = lax.psum(partial_rot, "tensor")
     in_proj = jnp.dot(
-        lax.all_gather(inputs, "tensor", axis=0, tiled=True),
-        in_side,
-        preferred_element_type=jnp.float32,
+        all_by_exchange(inputs, "tensor", 0), in_side, preferred_element_type=jnp.float32
     ).astype(jnp.bfloat16)
     piece = lax.all_gather(out_grad, "tensor", axis=0, tiled=True)
     hidden_rows = lax.dot_general(

time: 636 us -> 614 us (0.965)
  waiting for transfers between devices: 580 us -> 552 us
    all_gather x1 -> x0, waiting for transfers between devices: 31.7 us -> none  [on_device(): lax.all_gather(inputs, 'tensor', axis=0, tiled=True)]
    all_to_all x0 -> x1, waiting for transfers between devices: none -> 26.4 us  [all_by_exchange(): blocks = lax.all_to_all(blocks, axis, split_axis=0, concat_axis=0)]
    all_gather x1, waiting for transfers between devices: 34.8 us -> 11.9 us  [on_device(): piece = lax.all_gather(out_grad, 'tensor', axis=0, tiled=True)]
where the time goes in v1:
time: 614 us
  waiting for transfers between devices  552 us (90%)
  matrix products  31.2 us (5%)
  between operations  13.9 us (2%)
  local copies, waits for them, and re-layouts  9.02 us (1%)
  starting transfers between devices  6.24 us (1%)
    reduce_scatter x1, waiting for transfers between devices, on_device(): summed = lax.psum_scatter(low_grad, 'dp', scatter_dimension=0, tiled=True)  214 us
    psum x1, waiting for transfers between devices, on_device(): rotation = lax.psum(partial_rot, 'tensor')  104 us
    all_gather x1, waiting for transfers between devices, on_device(): lax.all_gather(second_old, 'dp', axis=0, tiled=True)  102 us
    all_gather x1, waiting for transfers between devices, on_device(): lax.all_gather(first_old, 'dp', axis=0, tiled=True)  91.3 us
    all_to_all x1, waiting for transfers between devices, all_by_exchange(): blocks = lax.all_to_all(blocks, axis, split_axis=0, concat_axis=0)  26.4 us
  transfers between devices with their start and end apart: 6, of which 6 were waited for; matrix products, arithmetic and copies ran while one was open for 6% of the time, Pallas kernels for 0%

profile of v1, /device:TPU:8, one launch (start us, length us, event | category | flops | bytes accessed | tf_op | source)
XLA Modules:
  0.0 614.1 jit_solution(15698266077553360290)
XLA Ops:
  7.2 0.0 copy-start
  7.2 0.0 copy-start.2
  7.2 0.0 all-gather.6.cloned.1.call-start
  7.2 0.7 all-gather.6.cloned.1.call-update
  7.9 0.0 all-reduce.2.cloned.1.call-start
  8.0 0.1 copy-done
  8.1 2.2 fusion.27
  10.3 0.0 all-reduce.2.cloned.1.call-update
  10.3 0.0 all-gather.8.cloned.1.call-start
  10.4 0.7 all-gather.8.cloned.1.call-update
  11.1 0.0 copy-done.2
  11.1 1.6 stack.10
  12.7 5.9 all-to-all-start
  18.6 0.0 reduce-scatter.2.cloned.1.call-start
  18.6 5.8 copy.11
  24.5 26.4 %all-to-all-done = bf16[16,32,2304]{2,1,0:T(8,128)(2,1)S(1)} async-done(((bf16[16,32,2304]{2,1,0:T(8,128)(2,1)}), bf16[16,32,2304]{2,1,0:T(8,128)(2,1)S(1)}, u32[]{:S(2)}, u32[]{:S(2)}) %all-to-all-start) | async-done | bytes 2359328 | tf_op jit(solution)/shard_map/all_to_all | solution.py:12
  50.8 3.1 fusion.17
  53.9 0.0 copy-start.3
  54.0 11.9 %all-gather.6.cloned.1.call-done = bf16[512,2304]{1,0:T(8,128)(2,1)} async-done(((bf16[32,2304]{1,0:T(8,128)(2,1)}), bf16[512,2304]{1,0:T(8,128)(2,1)}) %all-gather.6.cloned.1.call-update) | async-done | bytes 2359312 | tf_op jit(solution)/shard_map/all_gather | solution.py:41
  65.8 6.5 %fusion.48 = f32[512,1152]{1,0:T(8,128)S(1)} fusion(bf16[512,2304]{1,0:T(8,128)(2,1)} %all-gather.6.cloned.1.call-done, bf16[1152,2304]{1,0:T(8,128)(2,1)} %param.13), kind=kOutput, calls=%fused_computation.60 | convolution fusion | flops 2717908992 | bytes 10027008 | tf_op jit(solution)/shard_map/dot_general | solution.py:42
  72.3 0.0 copy-start.4
  72.3 1.4 copy-done.4
  73.7 0.0 copy-done.3
  73.7 1.2 convolution_bitcast_fusion.1
  74.9 4.8 convolution_bitcast_fusion
  79.7 4.4 convolution_bitcast_fusion.2
  84.1 2.1 pad_maximum_fusion
  86.2 0.0 reduce-scatter.2.cloned.1.call-update
  86.2 0.2 all-gather.4.cloned.1.call-start
  86.4 0.4 all-gather.4.cloned.1.call-update
  86.8 104.0 %all-reduce.2.cloned.1.call-done = f32[3,256,256]{2,1,0:T(8,128)} async-done(((f32[3,256,256]{2,1,0:T(8,128)}), f32[3,256,256]{2,1,0:T(8,128)}) %all-reduce.2.cloned.1.call-update) | async-done | bytes 786448 | tf_op jit(solution)/shard_map/psum | solution.py:37
  190.8 102.3 %all-gather.8.cloned.1.call-done = f32[256,3,1152]{2,0,1:T(8,128)} async-done(((f32[16,3,1152]{2,0,1:T(8,128)}), f32[256,3,1152]{2,0,1:T(8,128)}) %all-gather.8.cloned.1.call-update) | async-done | bytes 3538960 | tf_op jit(solution)/shard_map/all_gather | solution.py:62
  293.1 214.0 %reduce-scatter.2.cloned.1.call-done = f32[16,3,1152]{2,0,1:T(8,128)} async-done(((f32[256,3,1152]{2,0,1:T(8,128)}), f32[16,3,1152]{2,0,1:T(8,128)}) %reduce-scatter.2.cloned.1.call-update) | async-done | bytes 221200 | tf_op jit(solution)/shard_map/reduce_scatter | solution.py:64
  507.2 0.0 copy-start.1
  507.2 4.5 fusion.16
  511.7 91.3 %all-gather.4.cloned.1.call-done = f32[256,3,1152]{2,0,1:T(8,128)} async-done(((f32[16,3,1152]{2,0,1:T(8,128)}), f32[256,3,1152]{2,0,1:T(8,128)}) %all-gather.4.cloned.1.call-update) | async-done | bytes 3538960 | tf_op jit(solution)/shard_map/all_gather | solution.py:61
  603.0 0.0 copy-done.1
  603.0 4.5 fusion.14
Async XLA Ops:
  7.2 0.9 copy-start
  7.2 3.9 copy-start.2
  7.2 58.6 %all-gather.6.cloned.1.call-start = ((), (), s32[]{:S(2)}) async-start(), calls=%async_computation.4 | async-start | bytes 2506752 | tf_op jit(solution)/shard_map/all_gather | solution.py:41
  7.9 182.9 %all-reduce.2.cloned.1.call-start = ((), (), s32[]{:S(2)}) async-start(), calls=%async_computation.2 | async-start | bytes 1572864 | tf_op jit(solution)/shard_map/psum | solution.py:37
  10.3 282.8 %all-gather.8.cloned.1.call-start = ((), (), s32[]{:S(2)}) async-start(), calls=%async_computation.6 | async-start | bytes 3760128 | tf_op jit(solution)/shard_map/all_gather | solution.py:62
  12.7 38.1 %all-to-all-start = ((bf16[16,32,2304]{2,1,0:T(8,128)(2,1)}), bf16[16,32,2304]{2,1,0:T(8,128)(2,1)S(1)}, u32[]{:S(2)}, u32[]{:S(2)}) async-start(bf16[16,32,2304]{2,1,0:T(8,128)(2,1)} %stack.10), calls=%async_computation | async-start | bytes 4718592 | tf_op jit(solution)/shard_map/all_to_all | solution.py:12
  18.6 488.6 %reduce-scatter.2.cloned.1.call-start = ((), (), s32[]{:S(2)}) async-start(), calls=%async_computation.5 | async-start | bytes 3760128 | tf_op jit(solution)/shard_map/reduce_scatter | solution.py:64
  53.9 19.7 %copy-start.3 = (bf16[512,1152]{1,0:T(8,128)(2,1)S(1)}, bf16[512,1152]{1,0:T(8,128)(2,1)}, u32[]{:S(2)}) copy-start(bf16[512,1152]{1,0:T(8,128)(2,1)} %param.11) | copy-start | bytes 3538948
  72.3 1.4 copy-start.4
  86.2 516.8 %all-gather.4.cloned.1.call-start = ((), (), s32[]{:S(2)}) async-start(), calls=%async_computation.3 | async-start | bytes 3760128 | tf_op jit(solution)/shard_map/all_gather | solution.py:61
  507.2 95.8 %copy-start.1 = (f32[16,3,1152]{2,0,1:T(8,128)S(1)}, f32[16,3,1152]{2,0,1:T(8,128)}, u32[]{:S(2)}) copy-start(f32[16,3,1152]{2,0,1:T(8,128)} %reduce-scatter.2.cloned.1.call-done) | copy-start | bytes 663556
Sparse Core Ops, SparseCore 0:
  9.8 55.9 all-gather.5
  68.4 122.3 all-reduce.1
  193.4 99.6 all-gather.7
  297.0 210.1 reduce-scatter.1
  509.6 93.3 all-gather.3

commit v2 on v0

--- a/solution.py
+++ b/solution.py
@@ -2,6 +2,7 @@
 import jax.numpy as jnp
 from jax import lax
 from jax.sharding import PartitionSpec as P
+from jax.lax import all_gather
 
 coeff = 0.7978845608028654
 
@@ -27,7 +28,8 @@
     slab = width // lax.axis_size("tensor")
     own_new = lax.dynamic_slice_in_dim(proj_new, lax.axis_index("tensor") * slab, slab, 0)
     partial_rot = jnp.einsum("dki,dkj->kij", own_new, proj_old, preferred_element_type=jnp.float32)
-    rotation = lax.psum(partial_rot, "tensor")
+    order_counts = lambda a0, mesh_name: jnp.sum(all_gather(a0, axis_name=mesh_name), axis=0)
+    rotation = order_counts(partial_rot, "tensor")
     in_proj = jnp.dot(
         lax.all_gather(inputs, "tensor", axis=0, tiled=True),
         in_side,

time: 636 us -> 585 us (0.920)
  waiting for transfers between devices: 580 us -> 523 us
    psum x1 -> x0, waiting for transfers between devices: 103 us -> none  [on_device(): rotation = lax.psum(partial_rot, 'tensor')]
    all_gather x0 -> x1, waiting for transfers between devices: none -> 55.5 us  [on_device(): all_gather(a0, axis_name=mesh_name)]
    all_gather x1, waiting for transfers between devices: 102 us -> 93.3 us  [on_device(): lax.all_gather(second_old, 'dp', axis=0, tiled=True)]
  transfers between devices with their start and end apart: 6 -> 6, of which waited for: 6 -> 6; matrix products, arithmetic and copies ran while one was open for 6% -> 7% of each run, Pallas kernels for 0% -> 0%
where the time goes in v2:
time: 585 us; the launch traced here: 584 us
  waiting for transfers between devices  523 us (89%)
  matrix products  31.9 us (5%)
  between operations  14.2 us (2%)
  other arithmetic  7.58 us (1%)
  local copies, waits for them, and re-layouts  7.26 us (1%)
    reduce_scatter x1, waiting for transfers between devices, on_device(): summed = lax.psum_scatter(low_grad, 'dp', scatter_dimension=0, tiled=True)  214 us
    all_gather x1, waiting for transfers between devices, on_device(): lax.all_gather(second_old, 'dp', axis=0, tiled=True)  93.3 us
    all_gather x1, waiting for transfers between devices, on_device(): lax.all_gather(first_old, 'dp', axis=0, tiled=True)  91.4 us
    all_gather x1, waiting for transfers between devices, on_device(): all_gather(a0, axis_name=mesh_name)  55.5 us
    all_gather x1, waiting for transfers between devices, on_device(): piece = lax.all_gather(out_grad, 'tensor', axis=0, tiled=True)  34.8 us
    all_gather x1, waiting for transfers between devices, on_device(): lax.all_gather(inputs, 'tensor', axis=0, tiled=True)  31.7 us
  transfers between devices with their start and end apart: 6, of which 6 were waited for; matrix products, arithmetic and copies ran while one was open for 7% of the time, Pallas kernels for 0%

profile of v2, /device:TPU:8, one launch (start us, length us, event | category | flops | bytes accessed | tf_op | source)
XLA Modules:
  0.0 584.4 jit_solution(127861698887139458)
XLA Ops:
  7.2 0.0 copy-start
  7.2 0.0 all-gather.9.cloned.1.call-start
  7.2 0.7 all-gather.9.cloned.1.call-update
  7.9 0.0 all-gather.11.cloned.1.call-start
  8.0 0.7 all-gather.11.cloned.1.call-update
  8.7 0.0 all-gather.15.cloned.1.call-start
  8.7 0.0 copy-done
  8.7 2.2 fusion.27
  11.0 0.0 all-gather.15.cloned.1.call-update
  11.0 0.0 all-gather.13.cloned.1.call-start
  11.0 0.5 all-gather.13.cloned.1.call-update
  11.6 0.0 reduce-scatter.2.cloned.1.call-start
  11.6 5.8 copy.12
  17.4 31.7 %all-gather.9.cloned.1.call-done = bf16[512,2304]{1,0:T(8,128)(2,1)} async-done(((bf16[32,2304]{1,0:T(8,128)(2,1)}), bf16[512,2304]{1,0:T(8,128)(2,1)}) %all-gather.9.cloned.1.call-update) | async-done | bytes 2359312 | tf_op jit(solution)/shard_map/all_gather | solution.py:34
  49.2 3.8 fusion.17
  53.0 0.0 copy-start.2
  53.0 34.8 %all-gather.11.cloned.1.call-done = bf16[512,2304]{1,0:T(8,128)(2,1)} async-done(((bf16[32,2304]{1,0:T(8,128)(2,1)}), bf16[512,2304]{1,0:T(8,128)(2,1)}) %all-gather.11.cloned.1.call-update) | async-done | bytes 2359312 | tf_op jit(solution)/shard_map/all_gather | solution.py:38
  87.8 6.5 %fusion.48 = f32[512,1152]{1,0:T(8,128)S(1)} fusion(bf16[512,2304]{1,0:T(8,128)(2,1)} %all-gather.11.cloned.1.call-done, bf16[1152,2304]{1,0:T(8,128)(2,1)} %param.13), kind=kOutput, calls=%fused_computation.60 | convolution fusion | flops 2717908992 | bytes 10027008 | tf_op jit(solution)/shard_map/dot_general | solution.py:39
  94.3 0.0 copy-start.3
  94.3 1.4 copy-done.3
  95.7 0.0 copy-done.2
  95.7 1.2 convolution_bitcast_fusion.1
  96.9 4.8 convolution_bitcast_fusion
  101.7 4.4 convolution_bitcast_fusion.2
  106.2 2.1 pad_maximum_fusion
  108.2 0.0 reduce-scatter.2.cloned.1.call-update
  108.2 0.2 all-gather.7.cloned.1.call-start
  108.5 0.3 all-gather.7.cloned.1.call-update
  108.8 55.5 %all-gather.15.cloned.1.call-done = f32[48,256,256]{2,1,0:T(8,128)} async-done(((f32[3,256,256]{2,1,0:T(8,128)}), f32[48,256,256]{2,1,0:T(8,128)}) %all-gather.15.cloned.1.call-update) | async-done | bytes 12582928 | tf_op jit(solution)/shard_map/all_gather | solution.py:31
  164.4 5.5 reduce_sum.9
  169.9 93.3 %all-gather.13.cloned.1.call-done = f32[256,3,1152]{2,0,1:T(8,128)} async-done(((f32[16,3,1152]{2,0,1:T(8,128)}), f32[256,3,1152]{2,0,1:T(8,128)}) %all-gather.13.cloned.1.call-update) | async-done | bytes 3538960 | tf_op jit(solution)/shard_map/all_gather | solution.py:59
  263.2 214.0 %reduce-scatter.2.cloned.1.call-done = f32[16,3,1152]{2,0,1:T(8,128)} async-done(((f32[256,3,1152]{2,0,1:T(8,128)}), f32[16,3,1152]{2,0,1:T(8,128)}) %reduce-scatter.2.cloned.1.call-update) | async-done | bytes 221200 | tf_op jit(solution)/shard_map/reduce_scatter | solution.py:61
  477.2 0.0 copy-start.1
  477.2 4.5 fusion.16
  481.7 91.4 %all-gather.7.cloned.1.call-done = f32[256,3,1152]{2,0,1:T(8,128)} async-done(((f32[16,3,1152]{2,0,1:T(8,128)}), f32[256,3,1152]{2,0,1:T(8,128)}) %all-gather.7.cloned.1.call-update) | async-done | bytes 3538960 | tf_op jit(solution)/shard_map/all_gather | solution.py:58
  573.0 0.0 copy-done.1
  573.0 4.5 fusion.14
Async XLA Ops:
  7.2 1.6 copy-start
  7.2 42.0 %all-gather.9.cloned.1.call-start = ((), (), s32[]{:S(2)}) async-start(), calls=%async_computation.2 | async-start | bytes 2506752 | tf_op jit(solution)/shard_map/all_gather | solution.py:34
  7.9 79.9 %all-gather.11.cloned.1.call-start = ((), (), s32[]{:S(2)}) async-start(), calls=%async_computation.3 | async-start | bytes 2506752 | tf_op jit(solution)/shard_map/all_gather | solution.py:38
  8.7 155.7 %all-gather.15.cloned.1.call-start = ((), (), s32[]{:S(2)}) async-start(), calls=%async_computation.6 | async-start | bytes 13369344 | tf_op jit(solution)/shard_map/all_gather | solution.py:31
  11.0 252.2 %all-gather.13.cloned.1.call-start = ((), (), s32[]{:S(2)}) async-start(), calls=%async_computation.5 | async-start | bytes 3760128 | tf_op jit(solution)/shard_map/all_gather | solution.py:59
  11.6 465.6 %reduce-scatter.2.cloned.1.call-start = ((), (), s32[]{:S(2)}) async-start(), calls=%async_computation.4 | async-start | bytes 3760128 | tf_op jit(solution)/shard_map/reduce_scatter | solution.py:61
  53.0 42.7 %copy-start.2 = (bf16[512,1152]{1,0:T(8,128)(2,1)S(1)}, bf16[512,1152]{1,0:T(8,128)(2,1)}, u32[]{:S(2)}) copy-start(bf16[512,1152]{1,0:T(8,128)(2,1)} %param.11) | copy-start | bytes 3538948
  94.3 1.4 copy-start.3
  108.2 464.8 %all-gather.7.cloned.1.call-start = ((), (), s32[]{:S(2)}) async-start(), calls=%async_computation.1 | async-start | bytes 3760128 | tf_op jit(solution)/shard_map/all_gather | solution.py:58
  477.2 95.9 %copy-start.1 = (f32[16,3,1152]{2,0,1:T(8,128)S(1)}, f32[16,3,1152]{2,0,1:T(8,128)}, u32[]{:S(2)}) copy-start(f32[16,3,1152]{2,0,1:T(8,128)} %reduce-scatter.2.cloned.1.call-done) | copy-start | bytes 663556
Sparse Core Ops, SparseCore 0:
  9.8 39.2 all-gather.8
  51.0 36.7 all-gather.10
  89.7 74.6 all-gather.14
  166.8 96.3 all-gather.12
  267.0 210.0 reduce-scatter.1
  479.6 93.3 all-gather.6
